TPU v7x, 32 devices: a whole 2x2x4 slice. The times are simulated.
32 devices in a mesh: leaf: 16 (over z, y, x), rhs: 2 (over core).
Axes of the slice: x: 2, y: 2, z: 4, core: 2. Of those that a mesh axis runs over, the one named last changes fastest.
Arguments:
- rhs_matrix: float32 [16384, 128], P('leaf', 'rhs'), may hold values from -21 to 21, as said below
- initial_guess: float32 [16384, 128], P('leaf', 'rhs'), may hold values from -4 to 4
- leaf_blocks: float32 [16384, 1024], P(('leaf', 'rhs')), may hold values from -2 to 8, as said below
- row_bases: float32 [4, 96, 16384], P(None, None, 'leaf'), may hold values from -1 to 1
- couplings: float32 [4, 96, 96], replicated, may hold values from -100 to 100, as said below
Outputs:
- solution: float32 [16384, 128], P('leaf', 'rhs')
- residual: float32 [16384, 128], P('leaf', 'rhs')
Inputs may be any that keep to these rules, and one draw needn't show every extreme that they name: `rhs_matrix`: column scales may differ; rows grow in scale toward the end of the rows. `leaf_blocks`: every 1024 x 1024 block is symmetric positive definite. `couplings`: every coupling matrix is symmetric positive definite.
All inputs are finite; a program needn't handle non-finite values.
Results may differ from a plain program's by a relative error of at most 0.0003.
Values sent between devices are 32-bit elements; how exact they have to be, the bound alone decides.
A program may use at most 64 MiB of HBM per device.

v0:
```python
import functools

import jax
import jax.numpy as jnp
from jax import lax
from jax.experimental import pallas as pl
from jax.experimental.pallas import tpu as pltpu
from jax.sharding import PartitionSpec as P

MESH = pl.DeviceIdType.MESH
F32 = jnp.float32
BF16 = jnp.bfloat16
LANES = 128
PIECES = 1
NN = (((1,), (0,)), ((), ()))
NT = (((1,), (1,)), ((), ()))


def halves(value):
    high = value.astype(BF16)
    return high, (value - high.astype(F32)).astype(BF16)


def dot3(left, right, dims):
    rows = left[0].shape[0]
    stacked = lax.dot_general(
        jnp.concatenate(left, axis=0), right[0], dims, preferred_element_type=F32
    )
    cross = lax.dot_general(left[0], right[1], dims, preferred_element_type=F32)
    return stacked[:rows] + (stacked[rows:] + cross)


def lane_fold(value):
    total = value[:, :LANES]
    for start in range(LANES, value.shape[1], LANES):
        total = total + value[:, start : start + LANES]
    return total


def kernel(
    x_hbm, b_hbm, d_hbm, u_hbm, c_hbm,
    r_ref, image_ref, step_ref,
    x_v, b_v, d_v, u_v, c_v,
    d_hi, d_lo, u_hi, u_lo, c_hi, c_lo, v_hi, v_lo, cc_hi, cc_lo,
    sums, base, z_in, w_out, w_in, t_out, t_in, s_out, s_in, q_out, q_in,
    local_sem, z_send, z_recv, w_send, w_recv, t_send, t_recv, s_send, s_recv, q_send, q_recv,
):
    tiers, rank, leaf = u_v.shape
    cols = x_v.shape[0]
    half = leaf // 2
    me, core = lax.axis_index("leaf"), lax.axis_index("rhs")
    other = 1 - core
    mine = pl.ds(pl.multiple_of(core * half, half), half)
    theirs = pl.ds(pl.multiple_of(other * half, half), half)

    def flip(leaf_index, stage):
        bit = 2**stage
        return leaf_index + bit * (1 - 2 * ((leaf_index // bit) % 2))

    def peer(stage):
        return (flip(me, stage), core)

    groups = [tuple(range(low, min(low + 2, tiers))) for low in range(0, tiers, 2)]
    group_peers = []
    for bits in groups:
        peers = [peer(stage) for stage in bits]
        if len(bits) == 2:
            peers.append((flip(flip(me, bits[0]), bits[1]), core))
        group_peers.append(peers)

    barrier = pltpu.get_barrier_semaphore()
    steps = groups

    def step_peers(step, tier):
        bits = steps[step]
        if len(bits) == 1 or tier < bits[1]:
            return [peer(bits[0])]
        return group_peers[bits[0] // 2]

    targets = [(me, other)] + [device for peers in group_peers for device in peers]
    for target in targets:
        pl.semaphore_signal(barrier, inc=1, device_id=target, device_id_type=MESH)

    tier_pairs = [slice(max(last - 2, 0), last) for last in range(tiers, 0, -2)]
    arrays = [(x_hbm, x_v)]
    arrays += [(u_hbm.at[pair], u_v.at[pair]) for pair in tier_pairs]
    arrays += [(d_hbm, d_v), (c_hbm, c_v), (b_hbm, b_v)]
    loads = [
        pltpu.make_async_copy(source, target, local_sem.at[index])
        for index, (source, target) in enumerate(arrays)
    ]
    for load in loads:
        load.start()
    x_load, *u_loads, d_load, c_load, b_load = loads

    def remote(source, target, send, recv, device):
        return pltpu.make_async_remote_copy(
            src_ref=source, dst_ref=target, send_sem=send, recv_sem=recv,
            device_id=device, device_id_type=MESH,
        )

    def z_copy(turn):
        source = x_hbm if turn == 0 else r_ref
        return remote(
            source.at[:, theirs], z_in.at[turn], z_send.at[turn], z_recv.at[turn], (me, other)
        )

    def w_copy(turn):
        return remote(
            w_out.at[turn], w_in.at[turn], w_send.at[turn], w_recv.at[turn], (me, other)
        )

    def pieces(tier):
        count = PIECES if tier >= tiers - 2 else 1
        size = cols // count
        return [(index, slice(index * size, (index + 1) * size)) for index in range(count)]

    def t_copy(turn, step, tier, piece, index):
        number, rows = piece
        out, into = (turn, step, tier, rows), (turn, step, tier, index, rows)
        sem = (turn, step, tier, index, number)
        return remote(
            t_out.at[out], t_in.at[into], t_send.at[sem], t_recv.at[sem], step_peers(step, tier)[index]
        )

    def send_tier(turn, step, tier, piece):
        for index in reversed(range(len(step_peers(step, tier)))):
            t_copy(turn, step, tier, piece, index).start()

    def s_copy(group, index):
        at = (group, index)
        return remote(
            s_out.at[group], s_in.at[at], s_send.at[at], s_recv.at[at], group_peers[group][index]
        )

    def q_copy(group):
        return remote(
            q_out.at[group], q_in.at[group], q_send.at[group], q_recv.at[group], group_peers[group][1]
        )

    padded = u_hi.shape[1]
    if padded > rank:
        blank = jnp.zeros((tiers, padded - rank, leaf), BF16)
        u_hi[:, rank:, :] = blank
        u_lo[:, rank:, :] = blank
    c_hi[...] = jnp.zeros_like(c_hi)
    c_lo[...] = jnp.zeros_like(c_lo)

    def project(turn):
        for index, pair in enumerate(tier_pairs):
            first, last = pair.start, pair.stop
            if turn == 0:
                u_loads[index].wait()
                for tier in range(first, last):
                    u_hi[tier, :rank], u_lo[tier, :rank] = halves(u_v[tier])
            bases = tuple(
                part[pair].reshape((last - first) * padded, leaf) for part in (u_hi, u_lo)
            )
            products = dot3((v_hi[...], v_lo[...]), bases, NT)
            for tier in range(first, last):
                start = (tier - first) * padded
                t_out[turn, 0, tier] = products[:, start : start + padded]
            if turn == 0 and index == 0:
                pl.semaphore_wait(barrier, len(targets))
            for tier in range(last - 1, first - 1, -1):
                for piece in pieces(tier):
                    send_tier(turn, 0, tier, piece)
            if turn == 0 and index == 0:
                z_copy(0).start()

    def combine(turn, step, tier):
        parts = []
        for piece in pieces(tier):
            rows = piece[1]
            part = t_out[turn, step, tier, rows]
            for index in range(len(step_peers(step, tier))):
                t_copy(turn, step, tier, piece, index).wait_recv()
                part = part + t_in[turn, step, tier, index, rows]
            if tier > steps[step][-1]:
                t_out[turn, step + 1, tier, rows] = part
                send_tier(turn, step + 1, tier, piece)
            parts.append(part)
        if tier > steps[step][-1]:
            return None
        total = jnp.concatenate(parts, axis=0)
        coupled = dot3(halves(total), (c_hi[tier], c_lo[tier]), NT)
        at = slice(tier * padded, (tier + 1) * padded)
        cc_hi[:, at], cc_lo[:, at] = halves(coupled)
        return lane_fold(total * coupled)

    def spread(first, last):
        at = slice(first * padded, last * padded)
        count = (last - first) * padded
        bases = tuple(part[first:last].reshape(count, leaf) for part in (u_hi, u_lo))
        return dot3((cc_hi[:, at], cc_lo[:, at]), bases, NN)

    def for_partner(turn):
        z_copy(turn).wait_recv()
        block = (d_hi[:, mine], d_lo[:, mine])
        w_out[turn] = dot3(halves(z_in[turn]), block, NT)
        w_copy(turn).start()

    def own_dense():
        sums[:, mine] = dot3((v_hi[...], v_lo[...]), (d_hi[...], d_lo[...]), NT)
        sums[:, theirs] = dot3(
            (v_hi[:, mine], v_lo[:, mine]), (d_hi[:, theirs], d_lo[:, theirs]), NN
        )

    def add_partner(turn):
        w_copy(turn).wait_recv()
        sums[:, theirs] = sums[:, theirs] + w_in[turn]

    x_load.wait()
    v_hi[...], v_lo[...] = halves(x_v[...])
    project(0)
    d_load.wait()
    d_hi[...], d_lo[...] = halves(d_v[...])
    for_partner(0)
    c_load.wait()
    c_hi[:, :rank, :rank], c_lo[:, :rank, :rank] = halves(c_v[...])
    low = steps[-1][0]
    for step, bits in enumerate(steps):
        if step == min(1, len(steps) - 1):
            own_dense()
        if step == len(steps) - 1:
            b_load.wait()
            add_partner(0)
            total = b_v[...] - sums[...]
            if low > 0:
                total = total - spread(0, low)
            base[...] = total
        for tier in range(tiers - 1, bits[0] - 1, -1):
            combine(0, step, tier)
    residual = base[...] - spread(low, tiers)
    r_ref[...] = residual
    z_copy(1).start()
    v_hi[...], v_lo[...] = halves(residual)

    project(1)
    own_dense()
    for_partner(1)

    def row_of(upper, lower):
        stacked = jnp.concatenate([upper, lower], axis=0)
        return jnp.sum(stacked.T, axis=0, keepdims=True)

    def start_sums(group, row):
        s_out[group] = jnp.broadcast_to(row, s_out.shape[1:])
        for index in range(len(group_peers[group])):
            s_copy(group, index).start()

    def start_quadratic(group, row):
        q_out[group] = jnp.broadcast_to(row, q_out.shape[1:])
        q_copy(group).start()

    def finish_sums(group):
        row = s_out[group, 0:1]
        for index in range(len(group_peers[group])):
            s_copy(group, index).wait_recv()
            row = row + s_in[group, index, 0:1]
        bits = groups[group]
        row = row + rows_found[bits[-1]]
        if len(bits) == 2:
            q_copy(group).wait_recv()
            row = row + (rows_found[bits[0]] + q_in[group, 0:1])
        return row

    rows_found = {}
    for step, bits in enumerate(steps):
        if step == len(steps) - 1 and low > 0:
            base[...] = sums[...] + spread(0, low)
        for tier in range(tiers - 1, bits[0] - 1, -1):
            found = combine(1, step, tier)
            if found is not None:
                rows_found[tier] = row_of(jnp.zeros_like(found), found)
                if tier != groups[tier // 2][-1]:
                    start_quadratic(tier // 2, rows_found[tier])
            if step > 0 and tier == tiers - 1:
                group = steps[step - 1][-1] // 2
                if steps[step - 1][-1] == groups[group][-1]:
                    start_sums(group + 1, finish_sums(group))
            if step == 0 and tier == max(tiers - 2, 0):
                add_partner(1)
                r_now = r_ref[...]
                start_sums(
                    0, row_of(lane_fold(r_now * r_now), lane_fold(r_now * sums[...]))
                )
    dense = base[...] if low > 0 else sums[...]
    image_ref[...] = dense + spread(low, tiers)
    row = finish_sums(len(groups) - 1)
    columns = jnp.broadcast_to(row, (row.shape[1], row.shape[1])).T
    step_ref[...] = columns[:cols] / columns[cols:]

    for turn in range(2):
        z_copy(turn).wait_send()
        w_copy(turn).wait_send()
        for step, bits in enumerate(steps):
            for tier in range(bits[0], tiers):
                for piece in pieces(tier):
                    for index in range(len(step_peers(step, tier))):
                        t_copy(turn, step, tier, piece, index).wait_send()
    for group, peers in enumerate(group_peers):
        for index in range(len(peers)):
            s_copy(group, index).wait_send()
        if len(groups[group]) == 2:
            q_copy(group).wait_send()


def finish(x_ref, r_ref, image_ref, step_ref, solution_ref, residual_ref):
    step = jnp.tile(step_ref[...], (1, x_ref.shape[1] // LANES))
    residual = r_ref[...]
    solution_ref[...] = x_ref[...] + step * residual
    residual_ref[...] = residual - step * image_ref[...]


def local(rhs_matrix, initial_guess, leaf_blocks, row_bases, couplings):
    tiers, rank, leaf = row_bases.shape
    cols = initial_guess.shape[1]
    half = leaf // 2
    groups = pl.cdiv(tiers, 2)
    padded = pl.cdiv(rank, LANES) * LANES
    assert 2 * cols == LANES and leaf_blocks.shape == (half, leaf)
    assert 2**tiers == lax.axis_size("leaf") and lax.axis_size("rhs") == 2
    any_spec = pl.BlockSpec(memory_space=pl.ANY)
    vmem_spec = pl.BlockSpec(memory_space=pltpu.VMEM)
    vmem, dma = pltpu.VMEM, pltpu.SemaphoreType.DMA
    guess = initial_guess.T
    residual, image, step = pl.pallas_call(
        kernel,
        out_shape=[
            jax.ShapeDtypeStruct((cols, leaf), F32),
            jax.ShapeDtypeStruct((cols, leaf), F32),
            jax.ShapeDtypeStruct((cols, LANES), F32),
        ],
        in_specs=[any_spec] * 5,
        out_specs=[vmem_spec] * 3,
        scratch_shapes=[
            vmem((cols, leaf), F32),
            vmem((cols, leaf), F32),
            vmem((half, leaf), F32),
            vmem((tiers, rank, leaf), F32),
            vmem((tiers, rank, rank), F32),
            vmem((half, leaf), BF16),
            vmem((half, leaf), BF16),
            vmem((tiers, padded, leaf), BF16),
            vmem((tiers, padded, leaf), BF16),
            vmem((tiers, padded, padded), BF16),
            vmem((tiers, padded, padded), BF16),
            vmem((cols, leaf), BF16),
            vmem((cols, leaf), BF16),
            vmem((cols, tiers * padded), BF16),
            vmem((cols, tiers * padded), BF16),
            vmem((cols, leaf), F32),
            vmem((cols, leaf), F32),
            vmem((2, cols, half), F32),
            vmem((2, cols, half), F32),
            vmem((2, cols, half), F32),
            vmem((2, tiers, tiers, cols, padded), F32),
            vmem((2, tiers, tiers, 3, cols, padded), F32),
            vmem((groups, 8, LANES), F32),
            vmem((groups, 3, 8, LANES), F32),
            vmem((groups, 8, LANES), F32),
            vmem((groups, 8, LANES), F32),
            dma((4 + groups,)),
            dma((2,)),
            dma((2,)),
            dma((2,)),
            dma((2,)),
            dma((2, tiers, tiers, 3, PIECES)),
            dma((2, tiers, tiers, 3, PIECES)),
            dma((groups, 3)),
            dma((groups, 3)),
            dma((groups,)),
            dma((groups,)),
        ],
        compiler_params=pltpu.CompilerParams(collective_id=0, has_side_effects=True),
        name="cg_step",
    )(guess, rhs_matrix.T, leaf_blocks, row_bases, couplings)
    ended = pl.pallas_call(
        finish,
        out_shape=[jax.ShapeDtypeStruct((cols, leaf), F32)] * 2,
        in_specs=[vmem_spec] * 4,
        out_specs=[vmem_spec] * 2,
        name="cg_update",
    )(guess, residual, image, step)
    return ended[0].T, ended[1].T


def solution(mesh):
    return jax.shard_map(
        local,
        mesh=mesh,
        in_specs=(
            P("leaf", "rhs"),
            P("leaf", "rhs"),
            P(("leaf", "rhs"), None),
            P(None, None, "leaf"),
            P(),
        ),
        out_specs=(P("leaf", "rhs"), P("leaf", "rhs")),
        check_vma=False,
    )
```

profile of v0, /device:TPU:0, one launch (start us, length us, event | category | flops | bytes accessed | tf_op | source)
XLA Modules:
  0.0 33.0 jit_solution(17378387614239590610)
XLA Ops:
  0.6 30.4 %cg_step.1 = (f32[64,1024]{1,0:T(8,128)}, f32[64,1024]{1,0:T(8,128)}, f32[64,128]{1,0:T(8,128)}) custom-call(f32[64,1024]{1,0:T(8,128)} %bitcast.4, f32[64,1024]{1,0:T(8,128)} %bitcast.6, f32[512,1024]{1,0:T(8,128)} %d_hbm.1, f32[4,96,1024]{2,1,0:T(8,128)} %u_hbm.1, f32[4,96,96]{2,1,0:T(8,128)} %c_hbm.1), custom_call_target="tpu_custom_call" | custom-call | tf_op jit(solution)/shard_map/cg_step/pallas_call | solution.py:328
  31.1 1.9 %cg_update.1 = (f32[64,1024]{1,0:T(8,128)}, f32[64,1024]{1,0:T(8,128)}) custom-call(f32[64,1024]{1,0:T(8,128)} %bitcast.5, f32[64,1024]{1,0:T(8,128)} %get-tuple-element.7.r_ref, f32[64,1024]{1,0:T(8,128)} %get-tuple-element.8.image_ref, f32[64,128]{1,0:T(8,128)} %get-tuple-element.9.step_ref), custom_call_target="tpu_custom_call" | custom-call | tf_op jit(solution)/shard_map/cg_update/pallas_call | solution.py:379
where the time goes:
time: 33.1 us; the launch traced here: 33 us
  Pallas kernels  32.3 us (98%)
  between operations  0.64 us (2%)
    pallas_call x1, Pallas kernels, local(): pl.pallas_call(kernel, out_shape=[jax.ShapeDtypeStruct((cols, leaf), F32)...  30.4 us
    pallas_call x1, Pallas kernels, local(): pl.pallas_call(finish, out_shape=[jax.ShapeDtypeStruct((cols, leaf), F32)...  1.94 us

commit v1 on v0

--- a/solution.py
+++ b/solution.py
@@ -306,13 +306,6 @@
             q_copy(group).wait_send()
 
 
-def finish(x_ref, r_ref, image_ref, step_ref, solution_ref, residual_ref):
-    step = jnp.tile(step_ref[...], (1, x_ref.shape[1] // LANES))
-    residual = r_ref[...]
-    solution_ref[...] = x_ref[...] + step * residual
-    residual_ref[...] = residual - step * image_ref[...]
-
-
 def local(rhs_matrix, initial_guess, leaf_blocks, row_bases, couplings):
     tiers, rank, leaf = row_bases.shape
     cols = initial_guess.shape[1]
@@ -327,11 +320,7 @@
     guess = initial_guess.T
     residual, image, step = pl.pallas_call(
         kernel,
-        out_shape=[
-            jax.ShapeDtypeStruct((cols, leaf), F32),
-            jax.ShapeDtypeStruct((cols, leaf), F32),
-            jax.ShapeDtypeStruct((cols, LANES), F32),
-        ],
+        out_shape=[vmem((cols, leaf), F32), vmem((cols, leaf), F32), vmem((cols, LANES), F32)],
         in_specs=[any_spec] * 5,
         out_specs=[vmem_spec] * 3,
         scratch_shapes=[
@@ -376,14 +365,8 @@
         compiler_params=pltpu.CompilerParams(collective_id=0, has_side_effects=True),
         name="cg_step",
     )(guess, rhs_matrix.T, leaf_blocks, row_bases, couplings)
-    ended = pl.pallas_call(
-        finish,
-        out_shape=[jax.ShapeDtypeStruct((cols, leaf), F32)] * 2,
-        in_specs=[vmem_spec] * 4,
-        out_specs=[vmem_spec] * 2,
-        name="cg_update",
-    )(guess, residual, image, step)
-    return ended[0].T, ended[1].T
+    alpha = jnp.tile(step, (1, leaf // LANES))
+    return (guess + alpha * residual).T, (residual - alpha * image).T
 
 
 def solution(mesh):

time: 33.1 us -> 31.3 us (0.946)
  Pallas kernels: 32.3 us -> 29.6 us
  other arithmetic: 0 us -> 0.89 us
    pallas_call x2 -> x1, Pallas kernels: 32.3 us -> 29.6 us  [local(): pl.pallas_call(kernel, out_shape=[vmem((cols, leaf), F32), vmem((cols, le...]
    transpose x0 -> x1, other arithmetic: none -> 0.89 us  [local(): return ((guess + alpha * residual).T, (residual - alpha * image).T)]
where the time goes in v1:
time: 31.3 us; the launch traced here: 31.2 us
  Pallas kernels  29.6 us (95%)
  other arithmetic  0.89 us (3%)
  between operations  0.66 us (2%)
    pallas_call x1, Pallas kernels, local(): pl.pallas_call(kernel, out_shape=[vmem((cols, leaf), F32), vmem((cols, le...  29.6 us
    transpose x1, other arithmetic, local(): return ((guess + alpha * residual).T, (residual - alpha * image).T)  0.89 us

profile of v1, /device:TPU:0, one launch (start us, length us, event | category | flops | bytes accessed | tf_op | source)
XLA Modules:
  0.0 31.2 jit_solution(9137084052540675575)
XLA Ops:
  0.6 0.0 copy-start
  0.6 29.6 %cg_step.1 = (f32[64,1024]{1,0:T(8,128)S(1)}, f32[64,1024]{1,0:T(8,128)S(1)}, f32[64,128]{1,0:T(8,128)S(1)}) custom-call(f32[64,1024]{1,0:T(8,128)} %bitcast.19, f32[64,1024]{1,0:T(8,128)} %bitcast.21, f32[512,1024]{1,0:T(8,128)} %d_hbm.1, f32[4,96,1024]{2,1,0:T(8,128)} %u_hbm.1, f32[4,96,96]{2,1,0:T(8,128)} %c_hbm.1), custom_call_target="tpu_custom_call" | custom-call | tf_op jit(solution)/shard_map/cg_step/pallas_call | solution.py:321
  30.3 0.0 copy-done
  30.3 0.9 %fusion.3 = (f32[1024,64]{0,1:T(8,128)}, f32[1024,64]{0,1:T(8,128)}) fusion(f32[64,1024]{1,0:T(8,128)S(1)} %get-tuple-element.6, f32[64,1024]{1,0:T(8,128)S(1)} %get-tuple-element.7, f32[8,8,8,128]{3,2,1,0:T(8,128)S(1)} %bitcast.20, f32[1024,64]{0,1:T(8,128)S(1)} %copy-done), kind=kLoop, calls=%fused_computation.5 | loop fusion | flops 262144 | bytes 1572864 | tf_op jit(solution)/shard_map/transpose | solution.py:369
  (1 shorter events, 0.0 us)
Async XLA Ops:
  0.6 29.7 %copy-start = (f32[1024,64]{0,1:T(8,128)S(1)}, f32[1024,64]{0,1:T(8,128)}, u32[]{:S(2)}) copy-start(f32[1024,64]{0,1:T(8,128)} %param.6) | copy-start | bytes 786436

commit v2 on v1

v2 whole, which is shorter than its diff:
```python
import functools

import jax
import jax.numpy as jnp
from jax import lax
from jax.experimental import pallas as pl
from jax.experimental.pallas import tpu as pltpu
from jax.sharding import PartitionSpec as P

MESH = pl.DeviceIdType.MESH
F32 = jnp.float32
BF16 = jnp.bfloat16
LANES = 128
DIRECT = 8
NN = (((1,), (0,)), ((), ()))
NT = (((1,), (1,)), ((), ()))


def halves(value):
    high = value.astype(BF16)
    return high, (value - high.astype(F32)).astype(BF16)


def dot3(left, right, dims):
    rows = left[0].shape[0]
    stacked = lax.dot_general(
        jnp.concatenate(left, axis=0), right[0], dims, preferred_element_type=F32
    )
    cross = lax.dot_general(left[0], right[1], dims, preferred_element_type=F32)
    return stacked[:rows] + (stacked[rows:] + cross)


def lane_fold(value):
    total = value[:, :LANES]
    for start in range(LANES, value.shape[1], LANES):
        total = total + value[:, start : start + LANES]
    return total


def masks_over(low, high):
    return [value << low for value in range(2 ** (high - low) - 1, 0, -1)]


def plan_of(tier):
    if 2 ** (tier + 1) <= DIRECT:
        return [masks_over(0, tier + 1)]
    return [masks_over(low, min(low + 2, tier + 1)) for low in range(0, tier + 1, 2)]


def flip(leaf_index, mask):
    bit = 1
    while bit <= mask:
        if mask & bit:
            leaf_index = leaf_index + bit * (1 - 2 * ((leaf_index // bit) % 2))
        bit *= 2
    return leaf_index


def pack_shape(cols, rank):
    padded = pl.cdiv(rank, LANES) * LANES
    spare = padded - rank
    if padded != LANES or not spare or rank % spare or cols * spare % (8 * LANES):
        return cols, padded
    return cols * rank // LANES, LANES


def pack(value, rank):
    cols, padded = value.shape
    keep = pack_shape(cols, rank)[0]
    if keep == cols:
        return value
    spare = padded - rank
    extra = value[keep:]
    moved = [
        pltpu.roll(extra, (rank - start) % padded, axis=1) for start in range(0, rank, spare)
    ]
    lane = lax.broadcasted_iota(jnp.int32, (keep, padded), 1)
    return jnp.where(lane < rank, value[:keep], jnp.concatenate(moved, axis=0))


def unpack(value, cols, rank):
    keep, padded = value.shape
    if keep == cols:
        return value
    spare = padded - rank
    count = cols - keep
    lane = lax.broadcasted_iota(jnp.int32, (count, padded), 1)
    extra = jnp.zeros((count, padded), F32)
    for index, start in enumerate(range(0, rank, spare)):
        part = pltpu.roll(
            value[index * count : (index + 1) * count], (start - rank) % padded, axis=1
        )
        extra = jnp.where((lane >= start) & (lane < start + spare), part, extra)
    lane = lax.broadcasted_iota(jnp.int32, (keep, padded), 1)
    return jnp.concatenate([jnp.where(lane < rank, value, 0.0), extra], axis=0)


def row_of(upper, lower):
    stacked = jnp.concatenate([upper, lower], axis=0)
    return jnp.sum(stacked.T, axis=0, keepdims=True)


def kernel(
    x_hbm, b_hbm, d_hbm, u_hbm, c_hbm,
    r_ref, image_ref, step_ref,
    x_v, b_v, d_v, e_v, u_v, c_v,
    d_hi, d_lo, e_hi, e_lo, u_hi, u_lo, c_hi, c_lo, w_hi, w_lo, v_hi, v_lo, cc_hi, cc_lo,
    sums, base, t_out, t_in, s_out, s_in, q_out, q_in,
    local_sem, e_send, e_recv, t_send, t_recv, s_send, s_recv, q_send, q_recv,
):
    tiers, rank, leaf = u_v.shape
    cols = x_v.shape[0]
    half = leaf // 2
    padded = u_hi.shape[1]
    me, core = lax.axis_index("leaf"), lax.axis_index("rhs")
    other = 1 - core
    mine = pl.ds(pl.multiple_of(core * half, half), half)
    theirs = pl.ds(pl.multiple_of(other * half, half), half)
    plans = [plan_of(tier) for tier in range(tiers)]
    low = sum(len(plan) == 1 for plan in plans)
    everyone = masks_over(0, tiers)

    barrier = pltpu.get_barrier_semaphore()
    for target in [(flip(me, mask), core) for mask in everyone] + [(me, other)]:
        pl.semaphore_signal(barrier, inc=1, device_id=target, device_id_type=MESH)

    arrays = [(x_hbm, x_v)]
    arrays += [(u_hbm.at[tier], u_v.at[tier]) for tier in reversed(range(tiers))]
    arrays += [(d_hbm, d_v), (c_hbm, c_v), (b_hbm, b_v)]
    loads = [
        pltpu.make_async_copy(source, target, local_sem.at[index])
        for index, (source, target) in enumerate(arrays)
    ]
    for load in loads:
        load.start()
    x_load, *u_loads, d_load, c_load, b_load = loads

    def remote(source, target, send, recv, device):
        return pltpu.make_async_remote_copy(
            src_ref=source, dst_ref=target, send_sem=send, recv_sem=recv,
            device_id=device, device_id_type=MESH,
        )

    e_copy = remote(d_hbm.at[:, mine], e_v, e_send, e_recv, (me, other))

    def t_copies(turn, tier, stage):
        at = (turn, tier, stage)
        return [
            remote(
                t_out.at[at], t_in.at[(*at, index)], t_send.at[at], t_recv.at[at],
                (flip(me, mask), core),
            )
            for index, mask in enumerate(plans[tier][stage])
        ]

    def s_copies():
        return [
            remote(s_out, s_in.at[index], s_send, s_recv, (flip(me, mask), core))
            for index, mask in enumerate(everyone)
        ]

    def q_copies(tier):
        return [
            remote(
                q_out.at[tier], q_in.at[tier, index], q_send.at[tier], q_recv.at[tier],
                (flip(me, mask), core),
            )
            for index, mask in enumerate(masks_over(tier + 1, tiers))
        ]

    def start(copies):
        for copy in copies:
            copy.start()

    def wait_all(buffer, sem):
        pltpu.make_async_copy(buffer, buffer, sem).wait()

    if padded > rank:
        blank = jnp.zeros((tiers, padded - rank, leaf), BF16)
        u_hi[:, rank:, :] = blank
        u_lo[:, rank:, :] = blank
    c_hi[...] = jnp.zeros_like(c_hi)
    c_lo[...] = jnp.zeros_like(c_lo)

    def project(turn, tier):
        products = dot3((v_hi[...], v_lo[...]), (u_hi[tier], u_lo[tier]), NT)
        t_out[turn, tier, 0] = pack(products, rank)

    def gathered(turn, tier, stage):
        count = len(plans[tier][stage])
        into = t_in.at[turn, tier, stage, :count]
        wait_all(into, t_recv.at[turn, tier, stage])
        return t_out[turn, tier, stage] + jnp.sum(into[...], axis=0)

    def forward(turn, tier, stage):
        t_out[turn, tier, stage + 1] = gathered(turn, tier, stage)
        start(t_copies(turn, tier, stage + 1))

    def total_of(turn, tier):
        return unpack(gathered(turn, tier, len(plans[tier]) - 1), cols, rank)

    def couple(tier, total):
        return dot3(total, (c_hi[tier], c_lo[tier]), NT)

    def place(tier, value):
        at = slice(tier * padded, (tier + 1) * padded)
        cc_hi[:, at], cc_lo[:, at] = value

    def spread(first, last, parts):
        at = slice(first * padded, last * padded)
        count = (last - first) * padded
        return dot3(
            (cc_hi[:, at], cc_lo[:, at]),
            tuple(part.reshape(count, leaf) for part in parts),
            NN,
        )

    def spread_low():
        return spread(0, low, (u_hi[:low], u_lo[:low]))

    def spread_high():
        return spread(low, tiers, (w_hi[...], w_lo[...]))

    def dense_own():
        sums[:, mine] = dot3((v_hi[...], v_lo[...]), (d_hi[...], d_lo[...]), NT)
        sums[:, theirs] = dot3(
            (v_hi[:, mine], v_lo[:, mine]), (d_hi[:, theirs], d_lo[:, theirs]), NN
        )

    def dense_rest():
        sums[:, theirs] = sums[:, theirs] + dot3(
            (v_hi[:, theirs], v_lo[:, theirs]), (e_hi[...], e_lo[...]), NN
        )

    stages = len(plans[-1])

    x_load.wait()
    v_hi[...], v_lo[...] = halves(x_v[...])
    for index, tier in enumerate(reversed(range(tiers))):
        u_loads[index].wait()
        u_hi[tier, :rank], u_lo[tier, :rank] = halves(u_v[tier])
        project(0, tier)
        if index == 0:
            pl.semaphore_wait(barrier, len(everyone) + 1)
        start(t_copies(0, tier, 0))
        if index == 0:
            e_copy.start()
    d_load.wait()
    d_hi[...], d_lo[...] = halves(d_v[...])
    dense_own()
    c_load.wait()
    c_hi[:, :rank, :rank], c_lo[:, :rank, :rank] = halves(c_v[...])
    for tier in range(low, tiers):
        w_hi[tier - low], w_lo[tier - low] = halves(
            dot3((c_hi[tier], c_lo[tier]), (u_hi[tier], u_lo[tier]), NN)
        )
    for stage in range(stages - 1):
        for tier in reversed(range(low, tiers)):
            if stage + 1 < len(plans[tier]):
                forward(0, tier, stage)
        if stage == 0:
            e_copy.wait_recv()
            e_hi[...], e_lo[...] = halves(e_v[...])
            dense_rest()
            b_load.wait()
            base[...] = b_v[...] - sums[...]
            for tier in range(low):
                place(tier, halves(couple(tier, halves(total_of(0, tier)))))
            base[...] = base[...] - spread_low()
    for tier in range(low, tiers):
        place(tier, halves(total_of(0, tier)))
    residual = base[...] - spread_high()
    r_ref[...] = residual
    v_hi[...], v_lo[...] = halves(residual)

    for tier in reversed(range(tiers)):
        project(1, tier)
        start(t_copies(1, tier, 0))
    dense_own()
    dense_rest()
    r_now = r_ref[...]
    rows = [row_of(lane_fold(r_now * r_now), lane_fold(r_now * sums[...]))]
    s_out[...] = jnp.broadcast_to(rows[0], s_out.shape)
    start(s_copies())

    def quadratic(tier, total):
        coupled = couple(tier, halves(total))
        found = lane_fold(total * coupled)
        rows.append(row_of(jnp.zeros_like(found), found))
        if tier < tiers - 1:
            q_out[tier] = jnp.broadcast_to(rows[-1], q_out.shape[1:])
            start(q_copies(tier))
        return coupled

    for stage in range(stages - 1):
        for tier in reversed(range(low, tiers)):
            if stage + 1 < len(plans[tier]):
                forward(1, tier, stage)
        if stage == 0:
            for tier in range(low):
                place(tier, halves(quadratic(tier, total_of(1, tier))))
            base[...] = sums[...] + spread_low()
    for tier in range(low, tiers):
        total = total_of(1, tier)
        place(tier, halves(total))
        quadratic(tier, total)
    image_ref[...] = base[...] + spread_high()
    wait_all(s_in, s_recv)
    row = jnp.sum(s_in[...], axis=0)
    for tier in range(tiers - 1):
        into = q_in.at[tier, : len(masks_over(tier + 1, tiers))]
        wait_all(into, q_recv.at[tier])
        row = row + jnp.sum(into[...], axis=0)
    row = row[:1] + sum(rows)
    columns = jnp.broadcast_to(row, (row.shape[1], row.shape[1])).T
    step_ref[...] = columns[:cols] / columns[cols:]

    e_copy.wait_send()
    for turn in range(2):
        for tier, plan in enumerate(plans):
            for stage in range(len(plan)):
                for copy in t_copies(turn, tier, stage):
                    copy.wait_send()
    for copy in s_copies():
        copy.wait_send()
    for tier in range(tiers - 1):
        for copy in q_copies(tier):
            copy.wait_send()


def local(rhs_matrix, initial_guess, leaf_blocks, row_bases, couplings):
    tiers, rank, leaf = row_bases.shape
    cols = initial_guess.shape[1]
    half = leaf // 2
    padded = pl.cdiv(rank, LANES) * LANES
    plans = [plan_of(tier) for tier in range(tiers)]
    low = sum(len(plan) == 1 for plan in plans)
    stages, most = len(plans[-1]), max(len(masks) for plan in plans for masks in plan)
    assert 2 * cols == LANES and leaf_blocks.shape == (half, leaf) and low < tiers
    assert 2**tiers == lax.axis_size("leaf") and lax.axis_size("rhs") == 2
    any_spec = pl.BlockSpec(memory_space=pl.ANY)
    vmem_spec = pl.BlockSpec(memory_space=pltpu.VMEM)
    vmem, dma = pltpu.VMEM, pltpu.SemaphoreType.DMA
    packed = pack_shape(cols, rank)
    guess = initial_guess.T
    residual, image, step = pl.pallas_call(
        kernel,
        out_shape=[vmem((cols, leaf), F32), vmem((cols, leaf), F32), vmem((cols, LANES), F32)],
        in_specs=[any_spec] * 5,
        out_specs=[vmem_spec] * 3,
        scratch_shapes=[
            vmem((cols, leaf), F32),
            vmem((cols, leaf), F32),
            vmem((half, leaf), F32),
            vmem((half, half), F32),
            vmem((tiers, rank, leaf), F32),
            vmem((tiers, rank, rank), F32),
            vmem((half, leaf), BF16),
            vmem((half, leaf), BF16),
            vmem((half, half), BF16),
            vmem((half, half), BF16),
            vmem((tiers, padded, leaf), BF16),
            vmem((tiers, padded, leaf), BF16),
            vmem((tiers, padded, padded), BF16),
            vmem((tiers, padded, padded), BF16),
            vmem((tiers - low, padded, leaf), BF16),
            vmem((tiers - low, padded, leaf), BF16),
            vmem((cols, leaf), BF16),
            vmem((cols, leaf), BF16),
            vmem((cols, tiers * padded), BF16),
            vmem((cols, tiers * padded), BF16),
            vmem((cols, leaf), F32),
            vmem((cols, leaf), F32),
            vmem((2, tiers, stages, *packed), F32),
            vmem((2, tiers, stages, most, *packed), F32),
            vmem((8, LANES), F32),
            vmem((2**tiers - 1, 8, LANES), F32),
            vmem((tiers, 8, LANES), F32),
            vmem((tiers, 2 ** (tiers - 1) - 1, 8, LANES), F32),
            dma((4 + tiers,)),
            dma,
            dma,
            dma((2, tiers, stages)),
            dma((2, tiers, stages)),
            dma,
            dma,
            dma((tiers,)),
            dma((tiers,)),
        ],
        compiler_params=pltpu.CompilerParams(collective_id=0, has_side_effects=True),
        name="cg_step",
    )(guess, rhs_matrix.T, leaf_blocks, row_bases, couplings)
    alpha = jnp.tile(step, (1, leaf // LANES))
    return (guess + alpha * residual).T, (residual - alpha * image).T


def solution(mesh):
    return jax.shard_map(
        local,
        mesh=mesh,
        in_specs=(
            P("leaf", "rhs"),
            P("leaf", "rhs"),
            P(("leaf", "rhs"), None),
            P(None, None, "leaf"),
            P(),
        ),
        out_specs=(P("leaf", "rhs"), P("leaf", "rhs")),
        check_vma=False,
    )
```

time: 31.3 us -> 27.4 us (0.88)
  Pallas kernels: 29.6 us -> 25.7 us
    pallas_call x1, Pallas kernels: 29.6 us -> 25.7 us  [local(): pl.pallas_call(kernel, out_shape=[vmem((cols, leaf), F32), vmem((cols, le...]
where the time goes in v2:
time: 27.4 us; the launch traced here: 27.3 us
  Pallas kernels  25.7 us (94%)
  other arithmetic  0.89 us (3%)
  between operations  0.66 us (2%)
    pallas_call x1, Pallas kernels, local(): pl.pallas_call(kernel, out_shape=[vmem((cols, leaf), F32), vmem((cols, le...  25.7 us
    transpose x1, other arithmetic, local(): return ((guess + alpha * residual).T, (residual - alpha * image).T)  0.89 us

profile of v2, /device:TPU:0, one launch (start us, length us, event | category | flops | bytes accessed | tf_op | source)
XLA Modules:
  0.0 27.3 jit_solution(14944352820003871269)
XLA Ops:
  0.6 0.0 copy-start
  0.6 25.7 %cg_step.1 = (f32[64,1024]{1,0:T(8,128)S(1)}, f32[64,1024]{1,0:T(8,128)S(1)}, f32[64,128]{1,0:T(8,128)S(1)}) custom-call(f32[64,1024]{1,0:T(8,128)} %bitcast.19, f32[64,1024]{1,0:T(8,128)} %bitcast.21, f32[512,1024]{1,0:T(8,128)} %d_hbm.1, f32[4,96,1024]{2,1,0:T(8,128)} %u_hbm.1, f32[4,96,96]{2,1,0:T(8,128)} %c_hbm.1), custom_call_target="tpu_custom_call" | custom-call | tf_op jit(solution)/shard_map/cg_step/pallas_call | solution.py:346
  26.4 0.0 copy-done
  26.4 0.9 %fusion.3 = (f32[1024,64]{0,1:T(8,128)}, f32[1024,64]{0,1:T(8,128)}) fusion(f32[64,1024]{1,0:T(8,128)S(1)} %get-tuple-element.6, f32[64,1024]{1,0:T(8,128)S(1)} %get-tuple-element.7, f32[8,8,8,128]{3,2,1,0:T(8,128)S(1)} %bitcast.20, f32[1024,64]{0,1:T(8,128)S(1)} %copy-done), kind=kLoop, calls=%fused_computation.5 | loop fusion | flops 262144 | bytes 1572864 | tf_op jit(solution)/shard_map/transpose | solution.py:394
  (1 shorter events, 0.0 us)
Async XLA Ops:
  0.6 25.8 %copy-start = (f32[1024,64]{0,1:T(8,128)S(1)}, f32[1024,64]{0,1:T(8,128)}, u32[]{:S(2)}) copy-start(f32[1024,64]{0,1:T(8,128)} %param.6) | copy-start | bytes 786436

commit v3 on v2

--- a/solution.py
+++ b/solution.py
@@ -237,7 +237,7 @@
     x_load.wait()
     v_hi[...], v_lo[...] = halves(x_v[...])
     for index, tier in enumerate(reversed(range(tiers))):
-        u_loads[index].wait()
+        u_loads[tiers - 1 - tier].wait()
         u_hi[tier, :rank], u_lo[tier, :rank] = halves(u_v[tier])
         project(0, tier)
         if index == 0:
@@ -273,14 +273,19 @@
     r_ref[...] = residual
     v_hi[...], v_lo[...] = halves(residual)
 
-    for tier in reversed(range(tiers)):
+    for tier in reversed(range(low, tiers)):
         project(1, tier)
+        start(t_copies(1, tier, 0))
+    blocks = tuple(part[:low].reshape(low * padded, leaf) for part in (u_hi, u_lo))
+    products = dot3((v_hi[...], v_lo[...]), blocks, NT)
+    for tier in range(low):
+        t_out[1, tier, 0] = pack(products[:, tier * padded : (tier + 1) * padded], rank)
         start(t_copies(1, tier, 0))
     dense_own()
     dense_rest()
     r_now = r_ref[...]
     rows = [row_of(lane_fold(r_now * r_now), lane_fold(r_now * sums[...]))]
-    s_out[...] = jnp.broadcast_to(rows[0], s_out.shape)
+    s_out[...] = rows[0]
     start(s_copies())
 
     def quadratic(tier, total):
@@ -288,7 +293,7 @@
         found = lane_fold(total * coupled)
         rows.append(row_of(jnp.zeros_like(found), found))
         if tier < tiers - 1:
-            q_out[tier] = jnp.broadcast_to(rows[-1], q_out.shape[1:])
+            q_out[tier] = rows[-1]
             start(q_copies(tier))
         return coupled
 
@@ -311,7 +316,7 @@
         into = q_in.at[tier, : len(masks_over(tier + 1, tiers))]
         wait_all(into, q_recv.at[tier])
         row = row + jnp.sum(into[...], axis=0)
-    row = row[:1] + sum(rows)
+    row = row + sum(rows)
     columns = jnp.broadcast_to(row, (row.shape[1], row.shape[1])).T
     step_ref[...] = columns[:cols] / columns[cols:]
 
@@ -373,10 +378,10 @@
             vmem((cols, leaf), F32),
             vmem((2, tiers, stages, *packed), F32),
             vmem((2, tiers, stages, most, *packed), F32),
-            vmem((8, LANES), F32),
-            vmem((2**tiers - 1, 8, LANES), F32),
-            vmem((tiers, 8, LANES), F32),
-            vmem((tiers, 2 ** (tiers - 1) - 1, 8, LANES), F32),
+            vmem((1, LANES), F32),
+            vmem((2**tiers - 1, 1, LANES), F32),
+            vmem((tiers, 1, LANES), F32),
+            vmem((tiers, 2 ** (tiers - 1) - 1, 1, LANES), F32),
             dma((4 + tiers,)),
             dma,
             dma,

time: 27.4 us -> 26.5 us (0.967)
  Pallas kernels: 25.7 us -> 24.8 us
    pallas_call x1, Pallas kernels: 25.7 us -> 24.8 us  [local(): pl.pallas_call(kernel, out_shape=[vmem((cols, leaf), F32), vmem((cols, le...]
where the time goes in v3:
time: 26.5 us; the launch traced here: 26.4 us
  Pallas kernels  24.8 us (94%)
  other arithmetic  0.89 us (3%)
  between operations  0.66 us (2%)
    pallas_call x1, Pallas kernels, local(): pl.pallas_call(kernel, out_shape=[vmem((cols, leaf), F32), vmem((cols, le...  24.8 us
    transpose x1, other arithmetic, local(): return ((guess + alpha * residual).T, (residual - alpha * image).T)  0.89 us

profile of v3, /device:TPU:0, one launch (start us, length us, event | category | flops | bytes accessed | tf_op | source)
XLA Modules:
  0.0 26.4 jit_solution(4646198085458534482)
XLA Ops:
  0.6 0.0 copy-start
  0.6 24.8 %cg_step.1 = (f32[64,1024]{1,0:T(8,128)S(1)}, f32[64,1024]{1,0:T(8,128)S(1)}, f32[64,128]{1,0:T(8,128)S(1)}) custom-call(f32[64,1024]{1,0:T(8,128)} %bitcast.19, f32[64,1024]{1,0:T(8,128)} %bitcast.21, f32[512,1024]{1,0:T(8,128)} %d_hbm.1, f32[4,96,1024]{2,1,0:T(8,128)} %u_hbm.1, f32[4,96,96]{2,1,0:T(8,128)} %c_hbm.1), custom_call_target="tpu_custom_call" | custom-call | tf_op jit(solution)/shard_map/cg_step/pallas_call | solution.py:351
  25.5 0.0 copy-done
  25.5 0.9 %fusion.3 = (f32[1024,64]{0,1:T(8,128)}, f32[1024,64]{0,1:T(8,128)}) fusion(f32[64,1024]{1,0:T(8,128)S(1)} %get-tuple-element.6, f32[64,1024]{1,0:T(8,128)S(1)} %get-tuple-element.7, f32[8,8,8,128]{3,2,1,0:T(8,128)S(1)} %bitcast.20, f32[1024,64]{0,1:T(8,128)S(1)} %copy-done), kind=kLoop, calls=%fused_computation.5 | loop fusion | flops 262144 | bytes 1572864 | tf_op jit(solution)/shard_map/transpose | solution.py:399
  (1 shorter events, 0.0 us)
Async XLA Ops:
  0.6 24.9 %copy-start = (f32[1024,64]{0,1:T(8,128)S(1)}, f32[1024,64]{0,1:T(8,128)}, u32[]{:S(2)}) copy-start(f32[1024,64]{0,1:T(8,128)} %param.6) | copy-start | bytes 786436

commit v4 on v3

--- a/solution.py
+++ b/solution.py
@@ -41,8 +41,8 @@
     return [value << low for value in range(2 ** (high - low) - 1, 0, -1)]
 
 
-def plan_of(tier):
-    if 2 ** (tier + 1) <= DIRECT:
+def plan_of(turn, tier):
+    if turn == 1 and 2 ** (tier + 1) <= DIRECT:
         return [masks_over(0, tier + 1)]
     return [masks_over(low, min(low + 2, tier + 1)) for low in range(0, tier + 1, 2)]
 
@@ -116,12 +116,13 @@
     other = 1 - core
     mine = pl.ds(pl.multiple_of(core * half, half), half)
     theirs = pl.ds(pl.multiple_of(other * half, half), half)
-    plans = [plan_of(tier) for tier in range(tiers)]
-    low = sum(len(plan) == 1 for plan in plans)
+    plans = [[plan_of(turn, tier) for tier in range(tiers)] for turn in range(2)]
+    first, low = [sum(len(plan) == 1 for plan in each) for each in plans]
     everyone = masks_over(0, tiers)
+    near = [mask for masks in plans[0][-1] for mask in reversed(masks)]
 
     barrier = pltpu.get_barrier_semaphore()
-    for target in [(flip(me, mask), core) for mask in everyone] + [(me, other)]:
+    for target in [(flip(me, mask), core) for mask in near] + [(me, other)]:
         pl.semaphore_signal(barrier, inc=1, device_id=target, device_id_type=MESH)
 
     arrays = [(x_hbm, x_v)]
@@ -150,7 +151,7 @@
                 t_out.at[at], t_in.at[(*at, index)], t_send.at[at], t_recv.at[at],
                 (flip(me, mask), core),
             )
-            for index, mask in enumerate(plans[tier][stage])
+            for index, mask in enumerate(plans[turn][tier][stage])
         ]
 
     def s_copies():
@@ -187,17 +188,21 @@
         t_out[turn, tier, 0] = pack(products, rank)
 
     def gathered(turn, tier, stage):
-        count = len(plans[tier][stage])
+        count = len(plans[turn][tier][stage])
         into = t_in.at[turn, tier, stage, :count]
         wait_all(into, t_recv.at[turn, tier, stage])
         return t_out[turn, tier, stage] + jnp.sum(into[...], axis=0)
 
+    def sent(turn, tier, stage):
+        count = len(plans[turn][tier][stage])
+        wait_all(t_in.at[turn, tier, stage, :count], t_send.at[turn, tier, stage])
+
     def forward(turn, tier, stage):
         t_out[turn, tier, stage + 1] = gathered(turn, tier, stage)
         start(t_copies(turn, tier, stage + 1))
 
     def total_of(turn, tier):
-        return unpack(gathered(turn, tier, len(plans[tier]) - 1), cols, rank)
+        return unpack(gathered(turn, tier, len(plans[turn][tier]) - 1), cols, rank)
 
     def couple(tier, total):
         return dot3(total, (c_hi[tier], c_lo[tier]), NT)
@@ -232,7 +237,7 @@
             (v_hi[:, theirs], v_lo[:, theirs]), (e_hi[...], e_lo[...]), NN
         )
 
-    stages = len(plans[-1])
+    stages = len(plans[0][-1])
 
     x_load.wait()
     v_hi[...], v_lo[...] = halves(x_v[...])
@@ -241,7 +246,7 @@
         u_hi[tier, :rank], u_lo[tier, :rank] = halves(u_v[tier])
         project(0, tier)
         if index == 0:
-            pl.semaphore_wait(barrier, len(everyone) + 1)
+            pl.semaphore_wait(barrier, len(near) + 1)
         start(t_copies(0, tier, 0))
         if index == 0:
             e_copy.start()
@@ -255,8 +260,8 @@
             dot3((c_hi[tier], c_lo[tier]), (u_hi[tier], u_lo[tier]), NN)
         )
     for stage in range(stages - 1):
-        for tier in reversed(range(low, tiers)):
-            if stage + 1 < len(plans[tier]):
+        for tier in reversed(range(first, tiers)):
+            if stage + 1 < len(plans[0][tier]):
                 forward(0, tier, stage)
         if stage == 0:
             e_copy.wait_recv()
@@ -264,9 +269,11 @@
             dense_rest()
             b_load.wait()
             base[...] = b_v[...] - sums[...]
-            for tier in range(low):
+            for tier in range(first):
                 place(tier, halves(couple(tier, halves(total_of(0, tier)))))
-            base[...] = base[...] - spread_low()
+    for tier in range(first, low):
+        place(tier, halves(couple(tier, halves(total_of(0, tier)))))
+    base[...] = base[...] - spread_low()
     for tier in range(low, tiers):
         place(tier, halves(total_of(0, tier)))
     residual = base[...] - spread_high()
@@ -299,12 +306,20 @@
 
     for stage in range(stages - 1):
         for tier in reversed(range(low, tiers)):
-            if stage + 1 < len(plans[tier]):
+            if stage + 1 < len(plans[1][tier]):
                 forward(1, tier, stage)
         if stage == 0:
             for tier in range(low):
                 place(tier, halves(quadratic(tier, total_of(1, tier))))
             base[...] = sums[...] + spread_low()
+    e_copy.wait_send()
+    for tier, plan in enumerate(plans[0]):
+        for stage in range(len(plan)):
+            sent(0, tier, stage)
+    for tier, plan in enumerate(plans[1]):
+        for stage in range(len(plan) - 1):
+            sent(1, tier, stage)
+    wait_all(s_in, s_send)
     for tier in range(low, tiers):
         total = total_of(1, tier)
         place(tier, halves(total))
@@ -320,17 +335,11 @@
     columns = jnp.broadcast_to(row, (row.shape[1], row.shape[1])).T
     step_ref[...] = columns[:cols] / columns[cols:]
 
-    e_copy.wait_send()
-    for turn in range(2):
-        for tier, plan in enumerate(plans):
-            for stage in range(len(plan)):
-                for copy in t_copies(turn, tier, stage):
-                    copy.wait_send()
-    for copy in s_copies():
-        copy.wait_send()
+    for tier in range(tiers):
+        sent(1, tier, len(plans[1][tier]) - 1)
     for tier in range(tiers - 1):
-        for copy in q_copies(tier):
-            copy.wait_send()
+        into = q_in.at[tier, : len(masks_over(tier + 1, tiers))]
+        wait_all(into, q_send.at[tier])
 
 
 def local(rhs_matrix, initial_guess, leaf_blocks, row_bases, couplings):
@@ -338,8 +347,8 @@
     cols = initial_guess.shape[1]
     half = leaf // 2
     padded = pl.cdiv(rank, LANES) * LANES
-    plans = [plan_of(tier) for tier in range(tiers)]
-    low = sum(len(plan) == 1 for plan in plans)
+    plans = [plan_of(turn, tier) for turn in range(2) for tier in range(tiers)]
+    low = sum(len(plan) == 1 for plan in plans[tiers:])
     stages, most = len(plans[-1]), max(len(masks) for plan in plans for masks in plan)
     assert 2 * cols == LANES and leaf_blocks.shape == (half, leaf) and low < tiers
     assert 2**tiers == lax.axis_size("leaf") and lax.axis_size("rhs") == 2

time: 26.5 us -> 25.2 us (0.951)
  Pallas kernels: 24.8 us -> 23.5 us
    pallas_call x1, Pallas kernels: 24.8 us -> 23.5 us  [local(): pl.pallas_call(kernel, out_shape=[vmem((cols, leaf), F32), vmem((cols, le...]
where the time goes in v4:
time: 25.2 us; the launch traced here: 25.1 us
  Pallas kernels  23.5 us (93%)
  other arithmetic  0.89 us (4%)
  between operations  0.66 us (3%)
    pallas_call x1, Pallas kernels, local(): pl.pallas_call(kernel, out_shape=[vmem((cols, leaf), F32), vmem((cols, le...  23.5 us
    transpose x1, other arithmetic, local(): return ((guess + alpha * residual).T, (residual - alpha * image).T)  0.89 us

profile of v4, /device:TPU:0, one launch (start us, length us, event | category | flops | bytes accessed | tf_op | source)
XLA Modules:
  0.0 25.1 jit_solution(3088035510140915578)
XLA Ops:
  0.6 0.0 copy-start
  0.6 23.5 %cg_step.1 = (f32[64,1024]{1,0:T(8,128)S(1)}, f32[64,1024]{1,0:T(8,128)S(1)}, f32[64,128]{1,0:T(8,128)S(1)}) custom-call(f32[64,1024]{1,0:T(8,128)} %bitcast.19, f32[64,1024]{1,0:T(8,128)} %bitcast.21, f32[512,1024]{1,0:T(8,128)} %d_hbm.1, f32[4,96,1024]{2,1,0:T(8,128)} %u_hbm.1, f32[4,96,96]{2,1,0:T(8,128)} %c_hbm.1), custom_call_target="tpu_custom_call" | custom-call | tf_op jit(solution)/shard_map/cg_step/pallas_call | solution.py:360
  24.2 0.0 copy-done
  24.2 0.9 %fusion.3 = (f32[1024,64]{0,1:T(8,128)}, f32[1024,64]{0,1:T(8,128)}) fusion(f32[64,1024]{1,0:T(8,128)S(1)} %get-tuple-element.6, f32[64,1024]{1,0:T(8,128)S(1)} %get-tuple-element.7, f32[8,8,8,128]{3,2,1,0:T(8,128)S(1)} %bitcast.20, f32[1024,64]{0,1:T(8,128)S(1)} %copy-done), kind=kLoop, calls=%fused_computation.5 | loop fusion | flops 262144 | bytes 1572864 | tf_op jit(solution)/shard_map/transpose | solution.py:408
  (1 shorter events, 0.0 us)
Async XLA Ops:
  0.6 23.5 %copy-start = (f32[1024,64]{0,1:T(8,128)S(1)}, f32[1024,64]{0,1:T(8,128)}, u32[]{:S(2)}) copy-start(f32[1024,64]{0,1:T(8,128)} %param.6) | copy-start | bytes 786436

commit v5 on v4

--- a/solution.py
+++ b/solution.py
@@ -220,11 +220,13 @@
             NN,
         )
 
-    def spread_low():
-        return spread(0, low, (u_hi[:low], u_lo[:low]))
-
-    def spread_high():
-        return spread(low, tiers, (w_hi[...], w_lo[...]))
+    def spread_low(last):
+        return spread(0, last, (u_hi[:last], u_lo[:last]))
+
+    def spread_high(start_tier):
+        return spread(
+            start_tier, tiers, (w_hi[start_tier - first :], w_lo[start_tier - first :])
+        )
 
     def dense_own():
         sums[:, mine] = dot3((v_hi[...], v_lo[...]), (d_hi[...], d_lo[...]), NT)
@@ -255,8 +257,8 @@
     dense_own()
     c_load.wait()
     c_hi[:, :rank, :rank], c_lo[:, :rank, :rank] = halves(c_v[...])
-    for tier in range(low, tiers):
-        w_hi[tier - low], w_lo[tier - low] = halves(
+    for tier in range(first, tiers):
+        w_hi[tier - first], w_lo[tier - first] = halves(
             dot3((c_hi[tier], c_lo[tier]), (u_hi[tier], u_lo[tier]), NN)
         )
     for stage in range(stages - 1):
@@ -271,12 +273,10 @@
             base[...] = b_v[...] - sums[...]
             for tier in range(first):
                 place(tier, halves(couple(tier, halves(total_of(0, tier)))))
-    for tier in range(first, low):
-        place(tier, halves(couple(tier, halves(total_of(0, tier)))))
-    base[...] = base[...] - spread_low()
-    for tier in range(low, tiers):
+            base[...] = base[...] - spread_low(first)
+    for tier in range(first, tiers):
         place(tier, halves(total_of(0, tier)))
-    residual = base[...] - spread_high()
+    residual = base[...] - spread_high(first)
     r_ref[...] = residual
     v_hi[...], v_lo[...] = halves(residual)
 
@@ -311,7 +311,7 @@
         if stage == 0:
             for tier in range(low):
                 place(tier, halves(quadratic(tier, total_of(1, tier))))
-            base[...] = sums[...] + spread_low()
+            base[...] = sums[...] + spread_low(low)
     e_copy.wait_send()
     for tier, plan in enumerate(plans[0]):
         for stage in range(len(plan)):
@@ -324,7 +324,7 @@
         total = total_of(1, tier)
         place(tier, halves(total))
         quadratic(tier, total)
-    image_ref[...] = base[...] + spread_high()
+    image_ref[...] = base[...] + spread_high(low)
     wait_all(s_in, s_recv)
     row = jnp.sum(s_in[...], axis=0)
     for tier in range(tiers - 1):
@@ -348,7 +348,7 @@
     half = leaf // 2
     padded = pl.cdiv(rank, LANES) * LANES
     plans = [plan_of(turn, tier) for turn in range(2) for tier in range(tiers)]
-    low = sum(len(plan) == 1 for plan in plans[tiers:])
+    first, low = [sum(len(plan) == 1 for plan in each) for each in (plans[:tiers], plans[tiers:])]
     stages, most = len(plans[-1]), max(len(masks) for plan in plans for masks in plan)
     assert 2 * cols == LANES and leaf_blocks.shape == (half, leaf) and low < tiers
     assert 2**tiers == lax.axis_size("leaf") and lax.axis_size("rhs") == 2
@@ -377,8 +377,8 @@
             vmem((tiers, padded, leaf), BF16),
             vmem((tiers, padded, padded), BF16),
             vmem((tiers, padded, padded), BF16),
-            vmem((tiers - low, padded, leaf), BF16),
-            vmem((tiers - low, padded, leaf), BF16),
+            vmem((tiers - first, padded, leaf), BF16),
+            vmem((tiers - first, padded, leaf), BF16),
             vmem((cols, leaf), BF16),
             vmem((cols, leaf), BF16),
             vmem((cols, tiers * padded), BF16),

time: 25.2 us -> 25.1 us (level)
  no operation moved by 1% of the time
where the time goes in v5:
time: 25.1 us; the launch traced here: 24.9 us
  Pallas kernels  23.4 us (93%)
  other arithmetic  0.89 us (4%)
  between operations  0.66 us (3%)
    pallas_call x1, Pallas kernels, local(): pl.pallas_call(kernel, out_shape=[vmem((cols, leaf), F32), vmem((cols, le...  23.4 us
    transpose x1, other arithmetic, local(): return ((guess + alpha * residual).T, (residual - alpha * image).T)  0.89 us

profile of v5, /device:TPU:0, one launch (start us, length us, event | category | flops | bytes accessed | tf_op | source)
XLA Modules:
  0.0 24.9 jit_solution(16945498858105200689)
XLA Ops:
  0.6 0.0 copy-start
  0.6 23.4 %cg_step.1 = (f32[64,1024]{1,0:T(8,128)S(1)}, f32[64,1024]{1,0:T(8,128)S(1)}, f32[64,128]{1,0:T(8,128)S(1)}) custom-call(f32[64,1024]{1,0:T(8,128)} %bitcast.19, f32[64,1024]{1,0:T(8,128)} %bitcast.21, f32[512,1024]{1,0:T(8,128)} %d_hbm.1, f32[4,96,1024]{2,1,0:T(8,128)} %u_hbm.1, f32[4,96,96]{2,1,0:T(8,128)} %c_hbm.1), custom_call_target="tpu_custom_call" | custom-call | tf_op jit(solution)/shard_map/cg_step/pallas_call | solution.py:360
  24.0 0.0 copy-done
  24.0 0.9 %fusion.3 = (f32[1024,64]{0,1:T(8,128)}, f32[1024,64]{0,1:T(8,128)}) fusion(f32[64,1024]{1,0:T(8,128)S(1)} %get-tuple-element.6, f32[64,1024]{1,0:T(8,128)S(1)} %get-tuple-element.7, f32[8,8,8,128]{3,2,1,0:T(8,128)S(1)} %bitcast.20, f32[1024,64]{0,1:T(8,128)S(1)} %copy-done), kind=kLoop, calls=%fused_computation.5 | loop fusion | flops 262144 | bytes 1572864 | tf_op jit(solution)/shard_map/transpose | solution.py:408
  (1 shorter events, 0.0 us)
Async XLA Ops:
  0.6 23.4 %copy-start = (f32[1024,64]{0,1:T(8,128)S(1)}, f32[1024,64]{0,1:T(8,128)}, u32[]{:S(2)}) copy-start(f32[1024,64]{0,1:T(8,128)} %param.6) | copy-start | bytes 786436

commit v6 on v5

--- a/solution.py
+++ b/solution.py
@@ -45,6 +45,27 @@
     if turn == 1 and 2 ** (tier + 1) <= DIRECT:
         return [masks_over(0, tier + 1)]
     return [masks_over(low, min(low + 2, tier + 1)) for low in range(0, tier + 1, 2)]
+
+
+def layout_of(plans):
+    slots, counts = {}, []
+    for turn, each in enumerate(plans):
+        start_slot = sum(counts)
+        total = start_slot
+        for tier, plan in enumerate(each):
+            for stage, masks in enumerate(plan):
+                slots[turn, tier, stage] = total
+                total += len(masks)
+        counts.append(total - start_slot)
+    return slots, counts
+
+
+def row_layout(tiers):
+    places, total = [], 2**tiers - 1
+    for tier in range(tiers - 1):
+        places.append(total)
+        total += 2 ** (tiers - 1 - tier) - 1
+    return places, total
 
 
 def flip(leaf_index, mask):
@@ -105,8 +126,8 @@
     r_ref, image_ref, step_ref,
     x_v, b_v, d_v, e_v, u_v, c_v,
     d_hi, d_lo, e_hi, e_lo, u_hi, u_lo, c_hi, c_lo, w_hi, w_lo, v_hi, v_lo, cc_hi, cc_lo,
-    sums, base, t_out, t_in, s_out, s_in, q_out, q_in,
-    local_sem, e_send, e_recv, t_send, t_recv, s_send, s_recv, q_send, q_recv,
+    m_hi, m_lo, early, sums, base, t_out, t_in, row_out, row_in,
+    local_sem, e_send, e_recv, t_send, t_recv, row_send, row_recv,
 ):
     tiers, rank, leaf = u_v.shape
     cols = x_v.shape[0]
@@ -119,6 +140,9 @@
     plans = [[plan_of(turn, tier) for tier in range(tiers)] for turn in range(2)]
     first, low = [sum(len(plan) == 1 for plan in each) for each in plans]
     everyone = masks_over(0, tiers)
+    slots, counts = layout_of(plans)
+    gates = {key: index for index, key in enumerate(slots)}
+    places, _ = row_layout(tiers)
     near = [mask for masks in plans[0][-1] for mask in reversed(masks)]
 
     barrier = pltpu.get_barrier_semaphore()
@@ -126,7 +150,7 @@
         pl.semaphore_signal(barrier, inc=1, device_id=target, device_id_type=MESH)
 
     arrays = [(x_hbm, x_v)]
-    arrays += [(u_hbm.at[tier], u_v.at[tier]) for tier in reversed(range(tiers))]
+    arrays += [(u_hbm.at[part], u_v.at[part]) for part in (slice(tiers - 1, tiers), slice(0, tiers - 1))]
     arrays += [(d_hbm, d_v), (c_hbm, c_v), (b_hbm, b_v)]
     loads = [
         pltpu.make_async_copy(source, target, local_sem.at[index])
@@ -145,25 +169,25 @@
     e_copy = remote(d_hbm.at[:, mine], e_v, e_send, e_recv, (me, other))
 
     def t_copies(turn, tier, stage):
-        at = (turn, tier, stage)
+        key = (turn, tier, stage)
         return [
             remote(
-                t_out.at[at], t_in.at[(*at, index)], t_send.at[at], t_recv.at[at],
-                (flip(me, mask), core),
+                t_out.at[gates[key]], t_in.at[slots[key] + index],
+                t_send.at[turn], t_recv.at[gates[key]], (flip(me, mask), core),
             )
             for index, mask in enumerate(plans[turn][tier][stage])
         ]
 
     def s_copies():
         return [
-            remote(s_out, s_in.at[index], s_send, s_recv, (flip(me, mask), core))
+            remote(row_out.at[tiers - 1], row_in.at[index], row_send, row_recv, (flip(me, mask), core))
             for index, mask in enumerate(everyone)
         ]
 
     def q_copies(tier):
         return [
             remote(
-                q_out.at[tier], q_in.at[tier, index], q_send.at[tier], q_recv.at[tier],
+                row_out.at[tier], row_in.at[places[tier] + index], row_send, row_recv,
                 (flip(me, mask), core),
             )
             for index, mask in enumerate(masks_over(tier + 1, tiers))
@@ -185,20 +209,16 @@
 
     def project(turn, tier):
         products = dot3((v_hi[...], v_lo[...]), (u_hi[tier], u_lo[tier]), NT)
-        t_out[turn, tier, 0] = pack(products, rank)
+        t_out[gates[turn, tier, 0]] = pack(products, rank)
 
     def gathered(turn, tier, stage):
-        count = len(plans[turn][tier][stage])
-        into = t_in.at[turn, tier, stage, :count]
-        wait_all(into, t_recv.at[turn, tier, stage])
-        return t_out[turn, tier, stage] + jnp.sum(into[...], axis=0)
-
-    def sent(turn, tier, stage):
-        count = len(plans[turn][tier][stage])
-        wait_all(t_in.at[turn, tier, stage, :count], t_send.at[turn, tier, stage])
+        key = (turn, tier, stage)
+        into = t_in.at[slots[key] : slots[key] + len(plans[turn][tier][stage])]
+        wait_all(into, t_recv.at[gates[key]])
+        return t_out[gates[key]] + jnp.sum(into[...], axis=0)
 
     def forward(turn, tier, stage):
-        t_out[turn, tier, stage + 1] = gathered(turn, tier, stage)
+        t_out[gates[turn, tier, stage + 1]] = gathered(turn, tier, stage)
         start(t_copies(turn, tier, stage + 1))
 
     def total_of(turn, tier):
@@ -244,7 +264,8 @@
     x_load.wait()
     v_hi[...], v_lo[...] = halves(x_v[...])
     for index, tier in enumerate(reversed(range(tiers))):
-        u_loads[tiers - 1 - tier].wait()
+        if index < 2:
+            u_loads[index].wait()
         u_hi[tier, :rank], u_lo[tier, :rank] = halves(u_v[tier])
         project(0, tier)
         if index == 0:
@@ -261,6 +282,7 @@
         w_hi[tier - first], w_lo[tier - first] = halves(
             dot3((c_hi[tier], c_lo[tier]), (u_hi[tier], u_lo[tier]), NN)
         )
+    every = tuple(part[...].reshape(tiers * padded, leaf) for part in (u_hi, u_lo))
     for stage in range(stages - 1):
         for tier in reversed(range(first, tiers)):
             if stage + 1 < len(plans[0][tier]):
@@ -274,25 +296,25 @@
             for tier in range(first):
                 place(tier, halves(couple(tier, halves(total_of(0, tier)))))
             base[...] = base[...] - spread_low(first)
+            early[...] = dot3(halves(base[...]), every, NT)
+            count = (tiers - first) * padded
+            spreads = tuple(part[...].reshape(count, leaf) for part in (w_hi, w_lo))
+            m_hi[...], m_lo[...] = halves(dot3(spreads, every, NT))
     for tier in range(first, tiers):
         place(tier, halves(total_of(0, tier)))
+    late = slice(first * padded, tiers * padded)
+    products = early[...] - dot3((cc_hi[:, late], cc_lo[:, late]), (m_hi[...], m_lo[...]), NN)
+    for tier in [*reversed(range(low, tiers)), *range(low)]:
+        t_out[gates[1, tier, 0]] = pack(products[:, tier * padded : (tier + 1) * padded], rank)
+        start(t_copies(1, tier, 0))
     residual = base[...] - spread_high(first)
     r_ref[...] = residual
     v_hi[...], v_lo[...] = halves(residual)
-
-    for tier in reversed(range(low, tiers)):
-        project(1, tier)
-        start(t_copies(1, tier, 0))
-    blocks = tuple(part[:low].reshape(low * padded, leaf) for part in (u_hi, u_lo))
-    products = dot3((v_hi[...], v_lo[...]), blocks, NT)
-    for tier in range(low):
-        t_out[1, tier, 0] = pack(products[:, tier * padded : (tier + 1) * padded], rank)
-        start(t_copies(1, tier, 0))
     dense_own()
     dense_rest()
     r_now = r_ref[...]
     rows = [row_of(lane_fold(r_now * r_now), lane_fold(r_now * sums[...]))]
-    s_out[...] = rows[0]
+    row_out[tiers - 1] = rows[0]
     start(s_copies())
 
     def quadratic(tier, total):
@@ -300,7 +322,7 @@
         found = lane_fold(total * coupled)
         rows.append(row_of(jnp.zeros_like(found), found))
         if tier < tiers - 1:
-            q_out[tier] = rows[-1]
+            row_out[tier] = rows[-1]
             start(q_copies(tier))
         return coupled
 
@@ -313,33 +335,19 @@
                 place(tier, halves(quadratic(tier, total_of(1, tier))))
             base[...] = sums[...] + spread_low(low)
     e_copy.wait_send()
-    for tier, plan in enumerate(plans[0]):
-        for stage in range(len(plan)):
-            sent(0, tier, stage)
-    for tier, plan in enumerate(plans[1]):
-        for stage in range(len(plan) - 1):
-            sent(1, tier, stage)
-    wait_all(s_in, s_send)
+    wait_all(t_in.at[: counts[0]], t_send.at[0])
     for tier in range(low, tiers):
         total = total_of(1, tier)
         place(tier, halves(total))
         quadratic(tier, total)
     image_ref[...] = base[...] + spread_high(low)
-    wait_all(s_in, s_recv)
-    row = jnp.sum(s_in[...], axis=0)
-    for tier in range(tiers - 1):
-        into = q_in.at[tier, : len(masks_over(tier + 1, tiers))]
-        wait_all(into, q_recv.at[tier])
-        row = row + jnp.sum(into[...], axis=0)
-    row = row + sum(rows)
+    wait_all(row_in, row_recv)
+    row = jnp.sum(row_in[...], axis=0) + sum(rows)
     columns = jnp.broadcast_to(row, (row.shape[1], row.shape[1])).T
     step_ref[...] = columns[:cols] / columns[cols:]
 
-    for tier in range(tiers):
-        sent(1, tier, len(plans[1][tier]) - 1)
-    for tier in range(tiers - 1):
-        into = q_in.at[tier, : len(masks_over(tier + 1, tiers))]
-        wait_all(into, q_send.at[tier])
+    wait_all(t_in.at[counts[0] :], t_send.at[1])
+    wait_all(row_in, row_send)
 
 
 def local(rhs_matrix, initial_guess, leaf_blocks, row_bases, couplings):
@@ -347,9 +355,10 @@
     cols = initial_guess.shape[1]
     half = leaf // 2
     padded = pl.cdiv(rank, LANES) * LANES
-    plans = [plan_of(turn, tier) for turn in range(2) for tier in range(tiers)]
-    first, low = [sum(len(plan) == 1 for plan in each) for each in (plans[:tiers], plans[tiers:])]
-    stages, most = len(plans[-1]), max(len(masks) for plan in plans for masks in plan)
+    plans = [[plan_of(turn, tier) for tier in range(tiers)] for turn in range(2)]
+    first, low = [sum(len(plan) == 1 for plan in each) for each in plans]
+    slots, counts = layout_of(plans)
+    row_count = row_layout(tiers)[1]
     assert 2 * cols == LANES and leaf_blocks.shape == (half, leaf) and low < tiers
     assert 2**tiers == lax.axis_size("leaf") and lax.axis_size("rhs") == 2
     any_spec = pl.BlockSpec(memory_space=pl.ANY)
@@ -383,23 +392,22 @@
             vmem((cols, leaf), BF16),
             vmem((cols, tiers * padded), BF16),
             vmem((cols, tiers * padded), BF16),
+            vmem(((tiers - first) * padded, tiers * padded), BF16),
+            vmem(((tiers - first) * padded, tiers * padded), BF16),
+            vmem((cols, tiers * padded), F32),
             vmem((cols, leaf), F32),
             vmem((cols, leaf), F32),
-            vmem((2, tiers, stages, *packed), F32),
-            vmem((2, tiers, stages, most, *packed), F32),
-            vmem((1, LANES), F32),
-            vmem((2**tiers - 1, 1, LANES), F32),
+            vmem((len(slots), *packed), F32),
+            vmem((sum(counts), *packed), F32),
             vmem((tiers, 1, LANES), F32),
-            vmem((tiers, 2 ** (tiers - 1) - 1, 1, LANES), F32),
-            dma((4 + tiers,)),
+            vmem((row_count, 1, LANES), F32),
+            dma((6,)),
             dma,
             dma,
-            dma((2, tiers, stages)),
-            dma((2, tiers, stages)),
+            dma((2,)),
+            dma((len(slots),)),
             dma,
             dma,
-            dma((tiers,)),
-            dma((tiers,)),
         ],
         compiler_params=pltpu.CompilerParams(collective_id=0, has_side_effects=True),
         name="cg_step",

time: 25.1 us -> 24.7 us (0.984)
  Pallas kernels: 23.4 us -> 22.9 us
    pallas_call x1, Pallas kernels: 23.4 us -> 22.9 us  [local(): pl.pallas_call(kernel, out_shape=[vmem((cols, leaf), F32), vmem((cols, le...]
where the time goes in v6:
time: 24.7 us; the launch traced here: 24.5 us
  Pallas kernels  22.9 us (93%)
  other arithmetic  0.89 us (4%)
  between operations  0.66 us (3%)
    pallas_call x1, Pallas kernels, local(): pl.pallas_call(kernel, out_shape=[vmem((cols, leaf), F32), vmem((cols, le...  22.9 us
    transpose x1, other arithmetic, local(): return ((guess + alpha * residual).T, (residual - alpha * image).T)  0.89 us

profile of v6, /device:TPU:0, one launch (start us, length us, event | category | flops | bytes accessed | tf_op | source)
XLA Modules:
  0.0 24.5 jit_solution(13184415671625423043)
XLA Ops:
  0.6 0.0 copy-start
  0.6 22.9 %cg_step.1 = (f32[64,1024]{1,0:T(8,128)S(1)}, f32[64,1024]{1,0:T(8,128)S(1)}, f32[64,128]{1,0:T(8,128)S(1)}) custom-call(f32[64,1024]{1,0:T(8,128)} %bitcast.19, f32[64,1024]{1,0:T(8,128)} %bitcast.21, f32[512,1024]{1,0:T(8,128)} %d_hbm.1, f32[4,96,1024]{2,1,0:T(8,128)} %u_hbm.1, f32[4,96,96]{2,1,0:T(8,128)} %c_hbm.1), custom_call_target="tpu_custom_call" | custom-call | tf_op jit(solution)/shard_map/cg_step/pallas_call | solution.py:369
  23.6 0.0 copy-done
  23.6 0.9 %fusion.3 = (f32[1024,64]{0,1:T(8,128)}, f32[1024,64]{0,1:T(8,128)}) fusion(f32[64,1024]{1,0:T(8,128)S(1)} %get-tuple-element.6, f32[64,1024]{1,0:T(8,128)S(1)} %get-tuple-element.7, f32[8,8,8,128]{3,2,1,0:T(8,128)S(1)} %bitcast.20, f32[1024,64]{0,1:T(8,128)S(1)} %copy-done), kind=kLoop, calls=%fused_computation.5 | loop fusion | flops 262144 | bytes 1572864 | tf_op jit(solution)/shard_map/transpose | solution.py:416
  (1 shorter events, 0.0 us)
Async XLA Ops:
  0.6 23.0 %copy-start = (f32[1024,64]{0,1:T(8,128)S(1)}, f32[1024,64]{0,1:T(8,128)}, u32[]{:S(2)}) copy-start(f32[1024,64]{0,1:T(8,128)} %param.6) | copy-start | bytes 786436

commit v7 on v6

--- a/solution.py
+++ b/solution.py
@@ -123,8 +123,8 @@
 
 def kernel(
     x_hbm, b_hbm, d_hbm, u_hbm, c_hbm,
-    r_ref, image_ref, step_ref,
-    x_v, b_v, d_v, e_v, u_v, c_v,
+    r_ref, image_ref, step_ref, x_v,
+    b_v, d_v, e_v, u_v, c_v,
     d_hi, d_lo, e_hi, e_lo, u_hi, u_lo, c_hi, c_lo, w_hi, w_lo, v_hi, v_lo, cc_hi, cc_lo,
     m_hi, m_lo, early, sums, base, t_out, t_in, row_out, row_in,
     local_sem, e_send, e_recv, t_send, t_recv, row_send, row_recv,
@@ -173,7 +173,7 @@
         return [
             remote(
                 t_out.at[gates[key]], t_in.at[slots[key] + index],
-                t_send.at[turn], t_recv.at[gates[key]], (flip(me, mask), core),
+                t_send, t_recv.at[gates[key]], (flip(me, mask), core),
             )
             for index, mask in enumerate(plans[turn][tier][stage])
         ]
@@ -335,7 +335,6 @@
                 place(tier, halves(quadratic(tier, total_of(1, tier))))
             base[...] = sums[...] + spread_low(low)
     e_copy.wait_send()
-    wait_all(t_in.at[: counts[0]], t_send.at[0])
     for tier in range(low, tiers):
         total = total_of(1, tier)
         place(tier, halves(total))
@@ -346,7 +345,7 @@
     columns = jnp.broadcast_to(row, (row.shape[1], row.shape[1])).T
     step_ref[...] = columns[:cols] / columns[cols:]
 
-    wait_all(t_in.at[counts[0] :], t_send.at[1])
+    wait_all(t_in, t_send)
     wait_all(row_in, row_send)
 
 
@@ -366,13 +365,17 @@
     vmem, dma = pltpu.VMEM, pltpu.SemaphoreType.DMA
     packed = pack_shape(cols, rank)
     guess = initial_guess.T
-    residual, image, step = pl.pallas_call(
+    residual, image, step, held = pl.pallas_call(
         kernel,
-        out_shape=[vmem((cols, leaf), F32), vmem((cols, leaf), F32), vmem((cols, LANES), F32)],
+        out_shape=[
+            vmem((cols, leaf), F32),
+            vmem((cols, leaf), F32),
+            vmem((cols, LANES), F32),
+            vmem((cols, leaf), F32),
+        ],
         in_specs=[any_spec] * 5,
-        out_specs=[vmem_spec] * 3,
+        out_specs=[vmem_spec] * 4,
         scratch_shapes=[
-            vmem((cols, leaf), F32),
             vmem((cols, leaf), F32),
             vmem((half, leaf), F32),
             vmem((half, half), F32),
@@ -404,7 +407,7 @@
             dma((6,)),
             dma,
             dma,
-            dma((2,)),
+            dma,
             dma((len(slots),)),
             dma,
             dma,
@@ -413,7 +416,7 @@
         name="cg_step",
     )(guess, rhs_matrix.T, leaf_blocks, row_bases, couplings)
     alpha = jnp.tile(step, (1, leaf // LANES))
-    return (guess + alpha * residual).T, (residual - alpha * image).T
+    return (held + alpha * residual).T, (residual - alpha * image).T
 
 
 def solution(mesh):

time: 24.7 us -> 24.6 us (level)
  no operation moved by 1% of the time
where the time goes in v7:
time: 24.6 us; the launch traced here: 24.5 us
  Pallas kernels  22.9 us (93%)
  other arithmetic  0.89 us (4%)
  between operations  0.65 us (3%)
    pallas_call x1, Pallas kernels, local(): pl.pallas_call(kernel, out_shape=[vmem((cols, leaf), F32), vmem((cols, le...  22.9 us
    transpose x1, other arithmetic, local(): return ((held + alpha * residual).T, (residual - alpha * image).T)  0.89 us

profile of v7, /device:TPU:0, one launch (start us, length us, event | category | flops | bytes accessed | tf_op | source)
XLA Modules:
  0.0 24.5 jit_solution(4150671721970414193)
XLA Ops:
  0.6 22.9 %cg_step.1 = (f32[64,1024]{1,0:T(8,128)S(1)}, f32[64,1024]{1,0:T(8,128)S(1)}, f32[64,128]{1,0:T(8,128)S(1)}, f32[64,1024]{1,0:T(8,128)S(1)}) custom-call(f32[64,1024]{1,0:T(8,128)} %bitcast.19, f32[64,1024]{1,0:T(8,128)} %bitcast.20, f32[512,1024]{1,0:T(8,128)} %d_hbm.1, f32[4,96,1024]{2,1,0:T(8,128)} %u_hbm.1, f32[4,96,96]{2,1,0:T(8,128)} %c_hbm.1), custom_call_target="tpu_custom_call" | custom-call | tf_op jit(solution)/shard_map/cg_step/pallas_call | solution.py:368
  23.6 0.9 %fusion.3 = (f32[1024,64]{0,1:T(8,128)}, f32[1024,64]{0,1:T(8,128)}) fusion(f32[64,1024]{1,0:T(8,128)S(1)} %get-tuple-element.8, f32[64,1024]{1,0:T(8,128)S(1)} %get-tuple-element.9, f32[8,8,8,128]{3,2,1,0:T(8,128)S(1)} %bitcast.18, f32[64,1024]{1,0:T(8,128)S(1)} %get-tuple-element.6), kind=kLoop, calls=%fused_computation.5 | loop fusion | flops 262144 | bytes 1572864 | tf_op jit(solution)/shard_map/transpose | solution.py:419
  (1 shorter events, 0.0 us)

commit v8 on v7

--- a/solution.py
+++ b/solution.py
@@ -287,12 +287,13 @@
         for tier in reversed(range(first, tiers)):
             if stage + 1 < len(plans[0][tier]):
                 forward(0, tier, stage)
+            if stage == 0 and tier == tiers - 1:
+                e_copy.wait_recv()
+                e_hi[...], e_lo[...] = halves(e_v[...])
+                dense_rest()
+                b_load.wait()
+                base[...] = b_v[...] - sums[...]
         if stage == 0:
-            e_copy.wait_recv()
-            e_hi[...], e_lo[...] = halves(e_v[...])
-            dense_rest()
-            b_load.wait()
-            base[...] = b_v[...] - sums[...]
             for tier in range(first):
                 place(tier, halves(couple(tier, halves(total_of(0, tier)))))
             base[...] = base[...] - spread_low(first)
@@ -300,14 +301,25 @@
             count = (tiers - first) * padded
             spreads = tuple(part[...].reshape(count, leaf) for part in (w_hi, w_lo))
             m_hi[...], m_lo[...] = halves(dot3(spreads, every, NT))
-    for tier in range(first, tiers):
+    inner = (low - first) * padded
+    if inner:
+        for tier in range(first, low):
+            place(tier, halves(total_of(0, tier)))
+        at = slice(first * padded, low * padded)
+        early[...] = early[...] - dot3(
+            (cc_hi[:, at], cc_lo[:, at]), (m_hi[:inner], m_lo[:inner]), NN
+        )
+        base[...] = base[...] - spread(first, low, (w_hi[: low - first], w_lo[: low - first]))
+    for tier in range(low, tiers):
         place(tier, halves(total_of(0, tier)))
-    late = slice(first * padded, tiers * padded)
-    products = early[...] - dot3((cc_hi[:, late], cc_lo[:, late]), (m_hi[...], m_lo[...]), NN)
+    late = slice(low * padded, tiers * padded)
+    products = early[...] - dot3(
+        (cc_hi[:, late], cc_lo[:, late]), (m_hi[inner:], m_lo[inner:]), NN
+    )
     for tier in [*reversed(range(low, tiers)), *range(low)]:
         t_out[gates[1, tier, 0]] = pack(products[:, tier * padded : (tier + 1) * padded], rank)
         start(t_copies(1, tier, 0))
-    residual = base[...] - spread_high(first)
+    residual = base[...] - spread_high(low)
     r_ref[...] = residual
     v_hi[...], v_lo[...] = halves(residual)
     dense_own()

time: 24.6 us -> 24.9 us (1.012)
  Pallas kernels: 22.9 us -> 23.2 us
    pallas_call x1, Pallas kernels: 22.9 us -> 23.2 us  [local(): pl.pallas_call(kernel, out_shape=[vmem((cols, leaf), F32), vmem((cols, le...]
where the time goes in v8:
time: 24.9 us; the launch traced here: 24.7 us
  Pallas kernels  23.2 us (93%)
  other arithmetic  0.89 us (4%)
  between operations  0.65 us (3%)
    pallas_call x1, Pallas kernels, local(): pl.pallas_call(kernel, out_shape=[vmem((cols, leaf), F32), vmem((cols, le...  23.2 us
    transpose x1, other arithmetic, local(): return ((held + alpha * residual).T, (residual - alpha * image).T)  0.89 us

profile of v8, /device:TPU:0, one launch (start us, length us, event | category | flops | bytes accessed | tf_op | source)
XLA Modules:
  0.0 24.7 jit_solution(11845539143247019207)
XLA Ops:
  0.6 23.2 %cg_step.1 = (f32[64,1024]{1,0:T(8,128)S(1)}, f32[64,1024]{1,0:T(8,128)S(1)}, f32[64,128]{1,0:T(8,128)S(1)}, f32[64,1024]{1,0:T(8,128)S(1)}) custom-call(f32[64,1024]{1,0:T(8,128)} %bitcast.19, f32[64,1024]{1,0:T(8,128)} %bitcast.20, f32[512,1024]{1,0:T(8,128)} %d_hbm.1, f32[4,96,1024]{2,1,0:T(8,128)} %u_hbm.1, f32[4,96,96]{2,1,0:T(8,128)} %c_hbm.1), custom_call_target="tpu_custom_call" | custom-call | tf_op jit(solution)/shard_map/cg_step/pallas_call | solution.py:380
  23.8 0.9 %fusion.3 = (f32[1024,64]{0,1:T(8,128)}, f32[1024,64]{0,1:T(8,128)}) fusion(f32[64,1024]{1,0:T(8,128)S(1)} %get-tuple-element.8, f32[64,1024]{1,0:T(8,128)S(1)} %get-tuple-element.9, f32[8,8,8,128]{3,2,1,0:T(8,128)S(1)} %bitcast.18, f32[64,1024]{1,0:T(8,128)S(1)} %get-tuple-element.6), kind=kLoop, calls=%fused_computation.5 | loop fusion | flops 262144 | bytes 1572864 | tf_op jit(solution)/shard_map/transpose | solution.py:431
  (1 shorter events, 0.0 us)
